TPU v7x, 512 devices: a whole 4x4x16 slice. The times are simulated.
512 devices in a mesh: grp: 16 (over z), row: 32 (over x, y, core).
Axes of the slice: x: 4, y: 4, z: 16, core: 2. Of those that a mesh axis runs over, the one named last changes fastest.
Arguments:
- design: bfloat16 [786432, 512], P(('grp', 'row')), may hold values from -0.29882812 to 0.29882812
- scales: bfloat16 [786432], P(('grp', 'row')), may hold values from 0.3984375 to 9.5
- buckets: int32 [786432], P(('grp', 'row')), may hold values from 0 to 1535
Outputs:
- sketch: float32 [24576, 512], P(('grp', 'row'))
- precond: float32 [512, 512], P('grp')
All inputs are finite; a program needn't handle non-finite values.
Results may differ from a plain program's by a relative error of at most 0.0003.
Values sent between devices are 32-bit elements; how exact they have to be, the bound alone decides.
No kernel may reach another device: no remote copies, remote signals or barrier semaphores. Data moves between devices by JAX's collectives and lax.ppermute only.
A program may use at most 64 MiB of HBM per device.

v0:
```python
import jax
import jax.numpy as jnp
from jax import lax
from jax.sharding import PartitionSpec as P


def partner_2(block, axis, stride):
    count = lax.axis_size(axis)
    route = []
    for low in range(count):
        high = low | 1 << stride
        if high != low and high < count:
            route += [(low, high), (high, low)]
    return lax.ppermute(block, axis, route)


def chol_upper(gram_matrix):
    return jnp.linalg.cholesky(gram_matrix).T


def self_gram(matrix):
    return lax.dot_general(
        matrix,
        matrix,
        (((0,), (0,)), ((), ())),
        precision=lax.Precision.HIGHEST,
        preferred_element_type=jnp.float32,
    )


def per_device(design, scales, buckets):
    row_count = design.shape[0]
    col_count = design.shape[1]
    row_parts = lax.axis_size("row")
    owned_rows = row_count // row_parts
    label_ids = lax.iota(jnp.int32, row_count)
    onehot_table = jnp.where(
        label_ids[:, None] == buckets[None, :], scales[None, :], jnp.zeros((), jnp.bfloat16)
    )
    partial_value = jnp.dot(onehot_table, design, preferred_element_type=jnp.float32).reshape(
        row_parts, owned_rows, col_count
    )
    arrived = lax.all_to_all(partial_value, "row", split_axis=0, concat_axis=0, tiled=True)
    sketch = jnp.sum(arrived, axis=0)
    local_gram = self_gram(sketch)
    group_gram = lax.psum(local_gram, "row")
    factor = chol_upper(group_gram)
    for bit_index in range(lax.axis_size("grp").bit_length() - 1):
        partner = partner_2(factor, "grp", bit_index)
        factor = chol_upper(self_gram(factor) + self_gram(partner))
    precond = factor / jnp.sqrt(jnp.float32(row_count * lax.axis_size("grp")))
    slab_rows = col_count // lax.axis_size("grp")
    slab_start = lax.axis_index("grp") * slab_rows
    precond_rows = lax.dynamic_slice_in_dim(precond, slab_start, slab_rows, 0)
    return (sketch, precond_rows)


def solution(mesh):
    in_specs = (P(("grp", "row"), None), P(("grp", "row")), P(("grp", "row")))
    out_specs = (P(("grp", "row"), None), P("grp", None))
    return jax.shard_map(
        per_device, mesh=mesh, in_specs=in_specs, out_specs=out_specs, check_vma=False
    )
```

profile of v0, /device:TPU:1, one launch (start us, length us, event | category | flops | bytes accessed | tf_op | source)
XLA Modules:
  0.0 933.6 jit_solution(3870824916542653050)
XLA Ops:
  8.6 3.3 fusion.1
  11.9 49.7 %all_to_all.5 = f32[32,48,512]{2,1,0:T(8,128)} all-to-all(f32[32,48,512]{2,1,0:T(8,128)S(1)} %bitcast.130), channel_id=1, replica_groups=mesh['grp'=16,'row'=32] {'row'}, dimensions={0} | all-to-all | bytes 6291456 | tf_op jit(solution)/shard_map/all_to_all | solution.py:43
  61.6 2.1 reduce_sum.9
  63.7 2.1 fusion.158
  65.8 134.5 %all-reduce.3.cloned.1.call-done = f32[512,512]{0,1:T(8,128)} async-done(((f32[512,512]{0,1:T(8,128)}), f32[512,512]{0,1:T(8,128)}) %all-reduce.3.cloned.1.call-update) | async-done | bytes 1048592 | tf_op jit(solution)/shard_map/psum | solution.py:46
  200.3 1.6 copy.6
  201.9 1.4 fusion.10
  204.4 11.7 %cholesky.550 = f32[128,128]{1,0:T(8,128)S(1)} custom-call(f32[128,128]{1,0:T(8,128)S(1)} %cholesky.906), custom_call_target="Cholesky" | custom-call | tf_op jit(solution)/shard_map/jit(cholesky)/cholesky | solution.py:18
  216.2 9.8 %custom-call.32 = f32[1,128,128]{1,2,0:T(8,128)S(1)} custom-call(f32[1,128,128]{2,1,0:T(8,128)S(1)} %get-tuple-element.54), custom_call_target="InvertDiagBlocksLowerTriangular" | custom-call | tf_op jit(solution)/shard_map/jit(cholesky)/cholesky | solution.py:18
  228.6 12.1 %cholesky.569 = f32[128,128]{1,0:T(8,128)S(1)} custom-call(f32[128,128]{1,0:T(8,128)S(1)} %cholesky.910), custom_call_target="Cholesky" | custom-call | tf_op jit(solution)/shard_map/jit(cholesky)/cholesky | solution.py:18
  240.7 9.8 %custom-call.33 = f32[1,128,128]{1,2,0:T(8,128)S(1)} custom-call(f32[1,128,128]{2,1,0:T(8,128)S(1)} %get-tuple-element.51), custom_call_target="InvertDiagBlocksLowerTriangular" | custom-call | tf_op jit(solution)/shard_map/jit(cholesky)/cholesky | solution.py:18
  252.1 11.7 %cholesky.590 = f32[128,128]{1,0:T(8,128)S(1)} custom-call(f32[128,128]{1,0:T(8,128)S(1)} %cholesky.915), custom_call_target="Cholesky" | custom-call | tf_op jit(solution)/shard_map/jit(cholesky)/cholesky | solution.py:18
  264.6 9.8 %custom-call.34 = f32[1,128,128]{1,2,0:T(8,128)S(1)} custom-call(f32[1,128,128]{2,1,0:T(8,128)S(1)} %get-tuple-element.48), custom_call_target="InvertDiagBlocksLowerTriangular" | custom-call | tf_op jit(solution)/shard_map/jit(cholesky)/cholesky | solution.py:18
  275.8 11.9 %cholesky.607 = f32[128,128]{1,0:T(8,128)S(1)} custom-call(f32[128,128]{1,0:T(8,128)S(1)} %convolution_subtract_fusion.2), custom_call_target="Cholesky" | custom-call | tf_op jit(solution)/shard_map/jit(cholesky)/cholesky | solution.py:18
  291.8 3.2 collective-permute-start
  295.0 1.9 fusion.25
  296.9 20.7 %collective-permute-done = f32[512,512]{0,1:T(8,128)S(1)} collective-permute-done((f32[512,512]{0,1:T(8,128)S(1)}, f32[512,512]{0,1:T(8,128)S(1)}, u32[]{:S(2)}, u32[]{:S(2)}) %collective-permute-start) | collective-permute-done | bytes 1048608 | tf_op jit(solution)/shard_map/ppermute | solution.py:14
  317.6 1.9 convolution_add_fusion.3
  320.8 1.4 fusion.9
  323.2 11.7 %cholesky.622 = f32[128,128]{1,0:T(8,128)S(1)} custom-call(f32[128,128]{1,0:T(8,128)S(1)} %cholesky.919), custom_call_target="Cholesky" | custom-call | tf_op jit(solution)/shard_map/jit(cholesky)/cholesky | solution.py:18
  335.1 9.8 %custom-call.35 = f32[1,128,128]{1,2,0:T(8,128)S(1)} custom-call(f32[1,128,128]{2,1,0:T(8,128)S(1)} %get-tuple-element.44), custom_call_target="InvertDiagBlocksLowerTriangular" | custom-call | tf_op jit(solution)/shard_map/jit(cholesky)/cholesky | solution.py:18
  347.5 12.1 %cholesky.641 = f32[128,128]{1,0:T(8,128)S(1)} custom-call(f32[128,128]{1,0:T(8,128)S(1)} %cholesky.923), custom_call_target="Cholesky" | custom-call | tf_op jit(solution)/shard_map/jit(cholesky)/cholesky | solution.py:18
  360.9 9.8 %custom-call.36 = f32[1,128,128]{1,2,0:T(8,128)S(1)} custom-call(f32[1,128,128]{2,1,0:T(8,128)S(1)} %get-tuple-element.41), custom_call_target="InvertDiagBlocksLowerTriangular" | custom-call | tf_op jit(solution)/shard_map/jit(cholesky)/cholesky | solution.py:18
  372.3 11.7 %cholesky.662 = f32[128,128]{1,0:T(8,128)S(1)} custom-call(f32[128,128]{1,0:T(8,128)S(1)} %cholesky.928), custom_call_target="Cholesky" | custom-call | tf_op jit(solution)/shard_map/jit(cholesky)/cholesky | solution.py:18
  384.7 9.8 %custom-call.37 = f32[1,128,128]{1,2,0:T(8,128)S(1)} custom-call(f32[1,128,128]{2,1,0:T(8,128)S(1)} %get-tuple-element.38), custom_call_target="InvertDiagBlocksLowerTriangular" | custom-call | tf_op jit(solution)/shard_map/jit(cholesky)/cholesky | solution.py:18
  394.7 1.4 slice_subtract_fusion.11
  396.1 11.7 %cholesky.679 = f32[128,128]{1,0:T(8,128)S(1)} custom-call(f32[128,128]{1,0:T(8,128)S(1)} %slice_subtract_fusion.11), custom_call_target="Cholesky" | custom-call | tf_op jit(solution)/shard_map/jit(cholesky)/cholesky | solution.py:18
  411.3 4.2 collective-permute-start.1
  415.5 1.9 fusion.22
  417.4 43.2 %collective-permute-done.1 = f32[512,512]{0,1:T(8,128)S(1)} collective-permute-done((f32[512,512]{0,1:T(8,128)S(1)}, f32[512,512]{0,1:T(8,128)S(1)}, u32[]{:S(2)}, u32[]{:S(2)}) %collective-permute-start.1) | collective-permute-done | bytes 1048608 | tf_op jit(solution)/shard_map/ppermute | solution.py:14
  460.6 1.9 convolution_add_fusion.2
  463.8 1.4 fusion.8
  466.3 11.7 %cholesky.694 = f32[128,128]{1,0:T(8,128)S(1)} custom-call(f32[128,128]{1,0:T(8,128)S(1)} %cholesky.932), custom_call_target="Cholesky" | custom-call | tf_op jit(solution)/shard_map/jit(cholesky)/cholesky | solution.py:18
  478.1 9.8 %custom-call.38 = f32[1,128,128]{1,2,0:T(8,128)S(1)} custom-call(f32[1,128,128]{2,1,0:T(8,128)S(1)} %get-tuple-element.34), custom_call_target="InvertDiagBlocksLowerTriangular" | custom-call | tf_op jit(solution)/shard_map/jit(cholesky)/cholesky | solution.py:18
  490.5 12.1 %cholesky.713 = f32[128,128]{1,0:T(8,128)S(1)} custom-call(f32[128,128]{1,0:T(8,128)S(1)} %cholesky.936), custom_call_target="Cholesky" | custom-call | tf_op jit(solution)/shard_map/jit(cholesky)/cholesky | solution.py:18
  504.0 9.8 %custom-call.39 = f32[1,128,128]{1,2,0:T(8,128)S(1)} custom-call(f32[1,128,128]{2,1,0:T(8,128)S(1)} %get-tuple-element.31), custom_call_target="InvertDiagBlocksLowerTriangular" | custom-call | tf_op jit(solution)/shard_map/jit(cholesky)/cholesky | solution.py:18
  515.4 11.7 %cholesky.734 = f32[128,128]{1,0:T(8,128)S(1)} custom-call(f32[128,128]{1,0:T(8,128)S(1)} %cholesky.941), custom_call_target="Cholesky" | custom-call | tf_op jit(solution)/shard_map/jit(cholesky)/cholesky | solution.py:18
  527.7 9.8 %custom-call.40 = f32[1,128,128]{1,2,0:T(8,128)S(1)} custom-call(f32[1,128,128]{2,1,0:T(8,128)S(1)} %get-tuple-element.28), custom_call_target="InvertDiagBlocksLowerTriangular" | custom-call | tf_op jit(solution)/shard_map/jit(cholesky)/cholesky | solution.py:18
  539.2 11.7 %cholesky.751 = f32[128,128]{1,0:T(8,128)S(1)} custom-call(f32[128,128]{1,0:T(8,128)S(1)} %slice_subtract_fusion.10), custom_call_target="Cholesky" | custom-call | tf_op jit(solution)/shard_map/jit(cholesky)/cholesky | solution.py:18
  554.4 7.4 collective-permute-start.2
  561.8 1.9 fusion.19
  563.6 88.1 %collective-permute-done.2 = f32[512,512]{0,1:T(8,128)S(1)} collective-permute-done((f32[512,512]{0,1:T(8,128)S(1)}, f32[512,512]{0,1:T(8,128)S(1)}, u32[]{:S(2)}, u32[]{:S(2)}) %collective-permute-start.2) | collective-permute-done | bytes 1048608 | tf_op jit(solution)/shard_map/ppermute | solution.py:14
  651.7 1.9 convolution_add_fusion.1
  654.9 1.4 fusion.7
  657.4 11.7 %cholesky.766 = f32[128,128]{1,0:T(8,128)S(1)} custom-call(f32[128,128]{1,0:T(8,128)S(1)} %cholesky.945), custom_call_target="Cholesky" | custom-call | tf_op jit(solution)/shard_map/jit(cholesky)/cholesky | solution.py:18
  669.3 9.8 %custom-call.41 = f32[1,128,128]{1,2,0:T(8,128)S(1)} custom-call(f32[1,128,128]{2,1,0:T(8,128)S(1)} %get-tuple-element.24), custom_call_target="InvertDiagBlocksLowerTriangular" | custom-call | tf_op jit(solution)/shard_map/jit(cholesky)/cholesky | solution.py:18
  681.6 12.1 %cholesky.785 = f32[128,128]{1,0:T(8,128)S(1)} custom-call(f32[128,128]{1,0:T(8,128)S(1)} %cholesky.949), custom_call_target="Cholesky" | custom-call | tf_op jit(solution)/shard_map/jit(cholesky)/cholesky | solution.py:18
  695.1 9.8 %custom-call.42 = f32[1,128,128]{1,2,0:T(8,128)S(1)} custom-call(f32[1,128,128]{2,1,0:T(8,128)S(1)} %get-tuple-element.21), custom_call_target="InvertDiagBlocksLowerTriangular" | custom-call | tf_op jit(solution)/shard_map/jit(cholesky)/cholesky | solution.py:18
  706.5 11.7 %cholesky.806 = f32[128,128]{1,0:T(8,128)S(1)} custom-call(f32[128,128]{1,0:T(8,128)S(1)} %cholesky.954), custom_call_target="Cholesky" | custom-call | tf_op jit(solution)/shard_map/jit(cholesky)/cholesky | solution.py:18
  718.9 9.8 %custom-call.43 = f32[1,128,128]{1,2,0:T(8,128)S(1)} custom-call(f32[1,128,128]{2,1,0:T(8,128)S(1)} %get-tuple-element.18), custom_call_target="InvertDiagBlocksLowerTriangular" | custom-call | tf_op jit(solution)/shard_map/jit(cholesky)/cholesky | solution.py:18
  730.3 11.7 %cholesky.823 = f32[128,128]{1,0:T(8,128)S(1)} custom-call(f32[128,128]{1,0:T(8,128)S(1)} %slice_subtract_fusion.9), custom_call_target="Cholesky" | custom-call | tf_op jit(solution)/shard_map/jit(cholesky)/cholesky | solution.py:18
  746.5 11.1 %collective-permute-start.3 = (f32[512,512]{0,1:T(8,128)}, f32[512,512]{0,1:T(8,128)}, u32[]{:S(2)}, u32[]{:S(2)}) collective-permute-start(f32[512,512]{0,1:T(8,128)} %fusion.15), channel_id=1, source_target_pairs={{0,256},{256,0},{32,288},{288,32},{64,320},{320,64},{96,352},{352,... | collective-permute-start | bytes 3145736 | tf_op jit(solution)/shard_map/ppermute | solution.py:14
  757.7 1.9 fusion.16
  759.6 70.5 %collective-permute-done.3 = f32[512,512]{0,1:T(8,128)} collective-permute-done((f32[512,512]{0,1:T(8,128)}, f32[512,512]{0,1:T(8,128)}, u32[]{:S(2)}, u32[]{:S(2)}) %collective-permute-start.3) | collective-permute-done | bytes 1048608 | tf_op jit(solution)/shard_map/ppermute | solution.py:14
  830.0 3.5 convolution_add_fusion
  834.9 1.4 fusion.6
  837.3 11.7 %cholesky.838 = f32[128,128]{1,0:T(8,128)S(1)} custom-call(f32[128,128]{1,0:T(8,128)S(1)} %cholesky.958), custom_call_target="Cholesky" | custom-call | tf_op jit(solution)/shard_map/jit(cholesky)/cholesky | solution.py:18
  849.2 9.8 %custom-call.44 = f32[1,128,128]{1,2,0:T(8,128)S(1)} custom-call(f32[1,128,128]{2,1,0:T(8,128)S(1)} %get-tuple-element.14), custom_call_target="InvertDiagBlocksLowerTriangular" | custom-call | tf_op jit(solution)/shard_map/jit(cholesky)/cholesky | solution.py:18
  860.5 1.4 slice_subtract_fusion
  861.9 11.9 %cholesky.857 = f32[128,128]{1,0:T(8,128)S(1)} custom-call(f32[128,128]{1,0:T(8,128)S(1)} %cholesky.962), custom_call_target="Cholesky" | custom-call | tf_op jit(solution)/shard_map/jit(cholesky)/cholesky | solution.py:18
  875.2 9.8 %custom-call.45 = f32[1,128,128]{1,2,0:T(8,128)S(1)} custom-call(f32[1,128,128]{2,1,0:T(8,128)S(1)} %get-tuple-element.11), custom_call_target="InvertDiagBlocksLowerTriangular" | custom-call | tf_op jit(solution)/shard_map/jit(cholesky)/cholesky | solution.py:18
  886.6 11.7 %cholesky.878 = f32[128,128]{1,0:T(8,128)S(1)} custom-call(f32[128,128]{1,0:T(8,128)S(1)} %cholesky.967), custom_call_target="Cholesky" | custom-call | tf_op jit(solution)/shard_map/jit(cholesky)/cholesky | solution.py:18
  899.0 9.8 %custom-call.46 = f32[1,128,128]{1,2,0:T(8,128)S(1)} custom-call(f32[1,128,128]{2,1,0:T(8,128)S(1)} %get-tuple-element.8), custom_call_target="InvertDiagBlocksLowerTriangular" | custom-call | tf_op jit(solution)/shard_map/jit(cholesky)/cholesky | solution.py:18
  910.5 11.7 %cholesky.895 = f32[128,128]{1,0:T(8,128)S(1)} custom-call(f32[128,128]{1,0:T(8,128)S(1)} %slice_subtract_fusion.8), custom_call_target="Cholesky" | custom-call | tf_op jit(solution)/shard_map/jit(cholesky)/cholesky | solution.py:18
  (116 shorter events, 54.2 us)
Async XLA Ops:
  7.2 1.4 copy-start
  7.2 193.2 %all-reduce.3.cloned.1.call-start = ((), (), s32[]{:S(2)}) async-start(), calls=%async_computation.1 | async-start | bytes 2097152 | tf_op jit(solution)/shard_map/psum | solution.py:46
  63.7 139.6 %copy-start.6 = (f32[48,512]{1,0:T(8,128)}, f32[48,512]{1,0:T(8,128)S(1)}, u32[]{:S(2)}) copy-start(f32[48,512]{1,0:T(8,128)S(1)} %reduce_sum.9) | copy-start | bytes 294916
  203.4 1.0 copy-start.5
  291.8 25.8 %collective-permute-start = (f32[512,512]{0,1:T(8,128)S(1)}, f32[512,512]{0,1:T(8,128)S(1)}, u32[]{:S(2)}, u32[]{:S(2)}) collective-permute-start(f32[512,512]{0,1:T(8,128)S(1)} %fusion.24), channel_id=1, source_target_pairs={{0,32},{32,0},{64,96},{96,64},{128,160},{160,128},{192,224},{224,1... | collective-permute-start | bytes 3145736 | tf_op jit(solution)/shard_map/ppermute | solution.py:14
  322.2 1.0 copy-start.2
  411.3 49.3 %collective-permute-start.1 = (f32[512,512]{0,1:T(8,128)S(1)}, f32[512,512]{0,1:T(8,128)S(1)}, u32[]{:S(2)}, u32[]{:S(2)}) collective-permute-start(f32[512,512]{0,1:T(8,128)S(1)} %fusion.21), channel_id=1, source_target_pairs={{0,64},{64,0},{32,96},{96,32},{128,192},{192,128},{160,224},{224,1... | collective-permute-start | bytes 3145736 | tf_op jit(solution)/shard_map/ppermute | solution.py:14
  465.3 1.0 copy-start.3
  554.4 97.4 %collective-permute-start.2 = (f32[512,512]{0,1:T(8,128)S(1)}, f32[512,512]{0,1:T(8,128)S(1)}, u32[]{:S(2)}, u32[]{:S(2)}) collective-permute-start(f32[512,512]{0,1:T(8,128)S(1)} %fusion.18), channel_id=1, source_target_pairs={{0,128},{128,0},{32,160},{160,32},{64,192},{192,64},{96,224},{224,... | collective-permute-start | bytes 3145736 | tf_op jit(solution)/shard_map/ppermute | solution.py:14
  656.4 1.0 copy-start.4
  746.5 83.6 %collective-permute-start.3 = (f32[512,512]{0,1:T(8,128)}, f32[512,512]{0,1:T(8,128)}, u32[]{:S(2)}, u32[]{:S(2)}) collective-permute-start(f32[512,512]{0,1:T(8,128)} %fusion.15), channel_id=1, source_target_pairs={{0,256},{256,0},{32,288},{288,32},{64,320},{320,64},{96,352},{352,... | collective-permute-start | bytes 3145736 | tf_op jit(solution)/shard_map/ppermute | solution.py:14
  836.3 1.0 copy-start.1
Sparse Core Ops, SparseCore 0:
  65.9 134.3 all-reduce.2
where the time goes:
time: 938 us; the launch traced here: 934 us
  other arithmetic  408 us (43%)
  waiting for transfers between devices  357 us (38%)
  matrix products  50.3 us (5%)
  blocking collectives  49.7 us (5%)
  between operations  28 us (3%)
  starting transfers between devices  25.9 us (3%)
  local copies, waits for them, and re-layouts  14.7 us (2%)
    another operation x74, other arithmetic, chol_upper(): return jnp.linalg.cholesky(gram_matrix).T  397 us
    ppermute x4, waiting for transfers between devices, partner_2(): return lax.ppermute(block, axis, route)  222 us
    psum x1, waiting for transfers between devices, per_device(): group_gram = lax.psum(local_gram, 'row')  135 us
    all_to_all x1, blocking collectives, per_device(): lax.all_to_all(partial_value, 'row', split_axis=0, concat_axis=0, tiled=T...  49.7 us
    another operation x30, matrix products, chol_upper(): return jnp.linalg.cholesky(gram_matrix).T  28.3 us
    ppermute x4, starting transfers between devices, partner_2(): return lax.ppermute(block, axis, route)  25.8 us
  transfers between devices with their start and end apart: 5, of which 5 were waited for; matrix products, arithmetic and copies ran while one was open for 1% of the time, Pallas kernels for 0%

commit v1 on v0

--- a/solution.py
+++ b/solution.py
@@ -43,7 +43,11 @@
     arrived = lax.all_to_all(partial_value, "row", split_axis=0, concat_axis=0, tiled=True)
     sketch = jnp.sum(arrived, axis=0)
     local_gram = self_gram(sketch)
-    group_gram = lax.psum(local_gram, "row")
+    group_gram = local_gram
+    for hop in (1, 2, 4, 8, 16):
+        group_gram = group_gram + lax.ppermute(
+            group_gram, "row", [(dev, dev ^ hop) for dev in range(32)]
+        )
     factor = chol_upper(group_gram)
     for bit_index in range(lax.axis_size("grp").bit_length() - 1):
         partner = partner_2(factor, "grp", bit_index)

time: 938 us -> 900 us (0.959)
  waiting for transfers between devices: 357 us -> 319 us
  between operations: 28 us -> 14.8 us
  starting transfers between devices: 25.9 us -> 37.7 us
    psum x1 -> x0, waiting for transfers between devices: 135 us -> none  [per_device(): group_gram = lax.psum(local_gram, 'row')]
    ppermute x0 -> x5, waiting for transfers between devices: none -> 95.7 us  [per_device(): lax.ppermute(group_gram, 'row', [(dev, dev ^ hop) for dev in range(32)])]
    ppermute x0 -> x5, starting transfers between devices: none -> 12.3 us  [per_device(): lax.ppermute(group_gram, 'row', [(dev, dev ^ hop) for dev in range(32)])]
  transfers between devices with their start and end apart: 5 -> 9, of which waited for: 5 -> 9; matrix products, arithmetic and copies ran while one was open for 1% -> 1% of each run, Pallas kernels for 0% -> 0%
where the time goes in v1:
time: 900 us; the launch traced here: 894 us
  other arithmetic  409 us (45%)
  waiting for transfers between devices  319 us (35%)
  blocking collectives  49.7 us (6%)
  matrix products  49.3 us (5%)
  starting transfers between devices  37.7 us (4%)
  between operations  14.8 us (2%)
  local copies, waits for them, and re-layouts  14.6 us (2%)
    another operation x74, other arithmetic, chol_upper(): return jnp.linalg.cholesky(gram_matrix).T  397 us
    ppermute x4, waiting for transfers between devices, partner_2(): return lax.ppermute(block, axis, route)  223 us
    ppermute x5, waiting for transfers between devices, per_device(): lax.ppermute(group_gram, 'row', [(dev, dev ^ hop) for dev in range(32)])  95.7 us
    all_to_all x1, blocking collectives, per_device(): lax.all_to_all(partial_value, 'row', split_axis=0, concat_axis=0, tiled=T...  49.7 us
    another operation x30, matrix products, chol_upper(): return jnp.linalg.cholesky(gram_matrix).T  28.3 us
    ppermute x4, starting transfers between devices, partner_2(): return lax.ppermute(block, axis, route)  25.4 us
  transfers between devices with their start and end apart: 9, of which 9 were waited for; matrix products, arithmetic and copies ran while one was open for 1% of the time, Pallas kernels for 0%

profile of v1, /device:TPU:1, one launch (start us, length us, event | category | flops | bytes accessed | tf_op | source)
XLA Modules:
  0.0 893.8 jit_solution(500390742948371762)
XLA Ops:
  2.0 3.3 fusion.1
  5.4 49.7 %all_to_all.5 = f32[32,48,512]{2,1,0:T(8,128)} all-to-all(f32[32,48,512]{2,1,0:T(8,128)S(1)} %bitcast.130), channel_id=1, replica_groups=mesh['grp'=16,'row'=32] {'row'}, dimensions={0} | all-to-all | bytes 6291456 | tf_op jit(solution)/shard_map/all_to_all | solution.py:43
  55.1 2.1 reduce_sum.9
  58.2 2.0 collective-permute-start
  60.3 2.5 collective-permute-done
  63.0 1.9 collective-permute-start.1
  64.9 24.6 %collective-permute-done.1 = f32[512,512]{0,1:T(8,128)S(1)} collective-permute-done((f32[512,512]{0,1:T(8,128)S(1)}, f32[512,512]{0,1:T(8,128)S(1)}, u32[]{:S(2)}, u32[]{:S(2)}) %collective-permute-start.1) | collective-permute-done | bytes 1048608 | tf_op jit(solution)/shard_map/ppermute | solution.py:48
  89.7 3.0 collective-permute-start.2
  92.7 24.1 %collective-permute-done.2 = f32[512,512]{0,1:T(8,128)S(1)} collective-permute-done((f32[512,512]{0,1:T(8,128)S(1)}, f32[512,512]{0,1:T(8,128)S(1)}, u32[]{:S(2)}, u32[]{:S(2)}) %collective-permute-start.2) | collective-permute-done | bytes 1048608 | tf_op jit(solution)/shard_map/ppermute | solution.py:48
  117.0 1.9 collective-permute-start.3
  119.0 22.7 %collective-permute-done.3 = f32[512,512]{0,1:T(8,128)S(1)} collective-permute-done((f32[512,512]{0,1:T(8,128)S(1)}, f32[512,512]{0,1:T(8,128)S(1)}, u32[]{:S(2)}, u32[]{:S(2)}) %collective-permute-start.3) | collective-permute-done | bytes 1048608 | tf_op jit(solution)/shard_map/ppermute | solution.py:48
  141.9 3.4 collective-permute-start.4
  145.4 21.8 %collective-permute-done.4 = f32[512,512]{0,1:T(8,128)S(1)} collective-permute-done((f32[512,512]{0,1:T(8,128)S(1)}, f32[512,512]{0,1:T(8,128)S(1)}, u32[]{:S(2)}, u32[]{:S(2)}) %collective-permute-start.4) | collective-permute-done | bytes 1048608 | tf_op jit(solution)/shard_map/ppermute | solution.py:48
  171.2 11.7 %cholesky.550 = f32[128,128]{1,0:T(8,128)S(1)} custom-call(f32[128,128]{1,0:T(8,128)S(1)} %cholesky.906), custom_call_target="Cholesky" | custom-call | tf_op jit(solution)/shard_map/jit(cholesky)/cholesky | solution.py:18
  183.0 9.8 %custom-call.32 = f32[1,128,128]{1,2,0:T(8,128)S(1)} custom-call(f32[1,128,128]{2,1,0:T(8,128)S(1)} %get-tuple-element.54), custom_call_target="InvertDiagBlocksLowerTriangular" | custom-call | tf_op jit(solution)/shard_map/jit(cholesky)/cholesky | solution.py:18
  195.4 11.7 %cholesky.569 = f32[128,128]{1,0:T(8,128)S(1)} custom-call(f32[128,128]{1,0:T(8,128)S(1)} %cholesky.910), custom_call_target="Cholesky" | custom-call | tf_op jit(solution)/shard_map/jit(cholesky)/cholesky | solution.py:18
  207.1 10.2 %custom-call.33 = f32[1,128,128]{1,2,0:T(8,128)S(1)} custom-call(f32[1,128,128]{2,1,0:T(8,128)S(1)} %get-tuple-element.51), custom_call_target="InvertDiagBlocksLowerTriangular" | custom-call | tf_op jit(solution)/shard_map/jit(cholesky)/cholesky | solution.py:18
  218.9 11.7 %cholesky.590 = f32[128,128]{1,0:T(8,128)S(1)} custom-call(f32[128,128]{1,0:T(8,128)S(1)} %cholesky.915), custom_call_target="Cholesky" | custom-call | tf_op jit(solution)/shard_map/jit(cholesky)/cholesky | solution.py:18
  231.4 9.8 %custom-call.34 = f32[1,128,128]{1,2,0:T(8,128)S(1)} custom-call(f32[1,128,128]{2,1,0:T(8,128)S(1)} %get-tuple-element.48), custom_call_target="InvertDiagBlocksLowerTriangular" | custom-call | tf_op jit(solution)/shard_map/jit(cholesky)/cholesky | solution.py:18
  242.7 11.7 %cholesky.607 = f32[128,128]{1,0:T(8,128)S(1)} custom-call(f32[128,128]{1,0:T(8,128)S(1)} %slice_subtract_fusion.14), custom_call_target="Cholesky" | custom-call | tf_op jit(solution)/shard_map/jit(cholesky)/cholesky | solution.py:18
  258.7 1.9 collective-permute-start.5
  260.6 1.9 fusion.25
  262.5 19.0 %collective-permute-done.5 = f32[512,512]{0,1:T(8,128)S(1)} collective-permute-done((f32[512,512]{0,1:T(8,128)S(1)}, f32[512,512]{0,1:T(8,128)S(1)}, u32[]{:S(2)}, u32[]{:S(2)}) %collective-permute-start.5) | collective-permute-done | bytes 1048608 | tf_op jit(solution)/shard_map/ppermute | solution.py:14
  281.5 1.9 convolution_add_fusion.3
  287.1 11.7 %cholesky.622 = f32[128,128]{1,0:T(8,128)S(1)} custom-call(f32[128,128]{1,0:T(8,128)S(1)} %cholesky.919), custom_call_target="Cholesky" | custom-call | tf_op jit(solution)/shard_map/jit(cholesky)/cholesky | solution.py:18
  299.0 9.8 %custom-call.35 = f32[1,128,128]{1,2,0:T(8,128)S(1)} custom-call(f32[1,128,128]{2,1,0:T(8,128)S(1)} %get-tuple-element.44), custom_call_target="InvertDiagBlocksLowerTriangular" | custom-call | tf_op jit(solution)/shard_map/jit(cholesky)/cholesky | solution.py:18
  311.4 12.1 %cholesky.641 = f32[128,128]{1,0:T(8,128)S(1)} custom-call(f32[128,128]{1,0:T(8,128)S(1)} %cholesky.923), custom_call_target="Cholesky" | custom-call | tf_op jit(solution)/shard_map/jit(cholesky)/cholesky | solution.py:18
  324.8 9.8 %custom-call.36 = f32[1,128,128]{1,2,0:T(8,128)S(1)} custom-call(f32[1,128,128]{2,1,0:T(8,128)S(1)} %get-tuple-element.41), custom_call_target="InvertDiagBlocksLowerTriangular" | custom-call | tf_op jit(solution)/shard_map/jit(cholesky)/cholesky | solution.py:18
  336.2 11.7 %cholesky.662 = f32[128,128]{1,0:T(8,128)S(1)} custom-call(f32[128,128]{1,0:T(8,128)S(1)} %cholesky.928), custom_call_target="Cholesky" | custom-call | tf_op jit(solution)/shard_map/jit(cholesky)/cholesky | solution.py:18
  348.6 9.8 %custom-call.37 = f32[1,128,128]{1,2,0:T(8,128)S(1)} custom-call(f32[1,128,128]{2,1,0:T(8,128)S(1)} %get-tuple-element.38), custom_call_target="InvertDiagBlocksLowerTriangular" | custom-call | tf_op jit(solution)/shard_map/jit(cholesky)/cholesky | solution.py:18
  360.0 11.7 %cholesky.679 = f32[128,128]{1,0:T(8,128)S(1)} custom-call(f32[128,128]{1,0:T(8,128)S(1)} %slice_subtract_fusion.13), custom_call_target="Cholesky" | custom-call | tf_op jit(solution)/shard_map/jit(cholesky)/cholesky | solution.py:18
  375.2 3.5 collective-permute-start.6
  378.7 1.9 fusion.22
  380.6 44.8 %collective-permute-done.6 = f32[512,512]{0,1:T(8,128)S(1)} collective-permute-done((f32[512,512]{0,1:T(8,128)S(1)}, f32[512,512]{0,1:T(8,128)S(1)}, u32[]{:S(2)}, u32[]{:S(2)}) %collective-permute-start.6) | collective-permute-done | bytes 1048608 | tf_op jit(solution)/shard_map/ppermute | solution.py:14
  425.4 1.9 convolution_add_fusion.2
  431.0 11.7 %cholesky.694 = f32[128,128]{1,0:T(8,128)S(1)} custom-call(f32[128,128]{1,0:T(8,128)S(1)} %cholesky.932), custom_call_target="Cholesky" | custom-call | tf_op jit(solution)/shard_map/jit(cholesky)/cholesky | solution.py:18
  442.9 9.8 %custom-call.38 = f32[1,128,128]{1,2,0:T(8,128)S(1)} custom-call(f32[1,128,128]{2,1,0:T(8,128)S(1)} %get-tuple-element.34), custom_call_target="InvertDiagBlocksLowerTriangular" | custom-call | tf_op jit(solution)/shard_map/jit(cholesky)/cholesky | solution.py:18
  455.3 12.1 %cholesky.713 = f32[128,128]{1,0:T(8,128)S(1)} custom-call(f32[128,128]{1,0:T(8,128)S(1)} %cholesky.936), custom_call_target="Cholesky" | custom-call | tf_op jit(solution)/shard_map/jit(cholesky)/cholesky | solution.py:18
  468.7 9.8 %custom-call.39 = f32[1,128,128]{1,2,0:T(8,128)S(1)} custom-call(f32[1,128,128]{2,1,0:T(8,128)S(1)} %get-tuple-element.31), custom_call_target="InvertDiagBlocksLowerTriangular" | custom-call | tf_op jit(solution)/shard_map/jit(cholesky)/cholesky | solution.py:18
  480.1 11.7 %cholesky.734 = f32[128,128]{1,0:T(8,128)S(1)} custom-call(f32[128,128]{1,0:T(8,128)S(1)} %cholesky.941), custom_call_target="Cholesky" | custom-call | tf_op jit(solution)/shard_map/jit(cholesky)/cholesky | solution.py:18
  492.5 9.8 %custom-call.40 = f32[1,128,128]{1,2,0:T(8,128)S(1)} custom-call(f32[1,128,128]{2,1,0:T(8,128)S(1)} %get-tuple-element.28), custom_call_target="InvertDiagBlocksLowerTriangular" | custom-call | tf_op jit(solution)/shard_map/jit(cholesky)/cholesky | solution.py:18
  503.9 11.7 %cholesky.751 = f32[128,128]{1,0:T(8,128)S(1)} custom-call(f32[128,128]{1,0:T(8,128)S(1)} %slice_subtract_fusion.12), custom_call_target="Cholesky" | custom-call | tf_op jit(solution)/shard_map/jit(cholesky)/cholesky | solution.py:18
  519.1 7.1 collective-permute-start.7
  526.2 1.9 fusion.19
  528.1 88.3 %collective-permute-done.7 = f32[512,512]{0,1:T(8,128)S(1)} collective-permute-done((f32[512,512]{0,1:T(8,128)S(1)}, f32[512,512]{0,1:T(8,128)S(1)}, u32[]{:S(2)}, u32[]{:S(2)}) %collective-permute-start.7) | collective-permute-done | bytes 1048608 | tf_op jit(solution)/shard_map/ppermute | solution.py:14
  616.4 1.9 convolution_add_fusion.1
  622.0 11.7 %cholesky.766 = f32[128,128]{1,0:T(8,128)S(1)} custom-call(f32[128,128]{1,0:T(8,128)S(1)} %cholesky.945), custom_call_target="Cholesky" | custom-call | tf_op jit(solution)/shard_map/jit(cholesky)/cholesky | solution.py:18
  633.9 9.8 %custom-call.41 = f32[1,128,128]{1,2,0:T(8,128)S(1)} custom-call(f32[1,128,128]{2,1,0:T(8,128)S(1)} %get-tuple-element.24), custom_call_target="InvertDiagBlocksLowerTriangular" | custom-call | tf_op jit(solution)/shard_map/jit(cholesky)/cholesky | solution.py:18
  646.3 12.1 %cholesky.785 = f32[128,128]{1,0:T(8,128)S(1)} custom-call(f32[128,128]{1,0:T(8,128)S(1)} %cholesky.949), custom_call_target="Cholesky" | custom-call | tf_op jit(solution)/shard_map/jit(cholesky)/cholesky | solution.py:18
  659.7 9.8 %custom-call.42 = f32[1,128,128]{1,2,0:T(8,128)S(1)} custom-call(f32[1,128,128]{2,1,0:T(8,128)S(1)} %get-tuple-element.21), custom_call_target="InvertDiagBlocksLowerTriangular" | custom-call | tf_op jit(solution)/shard_map/jit(cholesky)/cholesky | solution.py:18
  671.1 11.7 %cholesky.806 = f32[128,128]{1,0:T(8,128)S(1)} custom-call(f32[128,128]{1,0:T(8,128)S(1)} %cholesky.954), custom_call_target="Cholesky" | custom-call | tf_op jit(solution)/shard_map/jit(cholesky)/cholesky | solution.py:18
  683.5 9.8 %custom-call.43 = f32[1,128,128]{1,2,0:T(8,128)S(1)} custom-call(f32[1,128,128]{2,1,0:T(8,128)S(1)} %get-tuple-element.18), custom_call_target="InvertDiagBlocksLowerTriangular" | custom-call | tf_op jit(solution)/shard_map/jit(cholesky)/cholesky | solution.py:18
  694.9 11.7 %cholesky.823 = f32[128,128]{1,0:T(8,128)S(1)} custom-call(f32[128,128]{1,0:T(8,128)S(1)} %slice_subtract_fusion.11), custom_call_target="Cholesky" | custom-call | tf_op jit(solution)/shard_map/jit(cholesky)/cholesky | solution.py:18
  711.1 12.9 %collective-permute-start.8 = (f32[512,512]{0,1:T(8,128)}, f32[512,512]{0,1:T(8,128)}, u32[]{:S(2)}, u32[]{:S(2)}) collective-permute-start(f32[512,512]{0,1:T(8,128)} %fusion.15), channel_id=1, source_target_pairs={{0,256},{256,0},{32,288},{288,32},{64,320},{320,64},{96,352},{352,... | collective-permute-start | bytes 3145736 | tf_op jit(solution)/shard_map/ppermute | solution.py:14
  724.1 1.9 fusion.16
  726.0 70.9 %collective-permute-done.8 = f32[512,512]{0,1:T(8,128)} collective-permute-done((f32[512,512]{0,1:T(8,128)}, f32[512,512]{0,1:T(8,128)}, u32[]{:S(2)}, u32[]{:S(2)}) %collective-permute-start.8) | collective-permute-done | bytes 1048608 | tf_op jit(solution)/shard_map/ppermute | solution.py:14
  796.9 3.5 convolution_add_fusion
  804.2 11.7 %cholesky.838 = f32[128,128]{1,0:T(8,128)S(1)} custom-call(f32[128,128]{1,0:T(8,128)S(1)} %cholesky.958), custom_call_target="Cholesky" | custom-call | tf_op jit(solution)/shard_map/jit(cholesky)/cholesky | solution.py:18
  816.1 9.8 %custom-call.44 = f32[1,128,128]{1,2,0:T(8,128)S(1)} custom-call(f32[1,128,128]{2,1,0:T(8,128)S(1)} %get-tuple-element.14), custom_call_target="InvertDiagBlocksLowerTriangular" | custom-call | tf_op jit(solution)/shard_map/jit(cholesky)/cholesky | solution.py:18
  828.8 11.9 %cholesky.857 = f32[128,128]{1,0:T(8,128)S(1)} custom-call(f32[128,128]{1,0:T(8,128)S(1)} %cholesky.962), custom_call_target="Cholesky" | custom-call | tf_op jit(solution)/shard_map/jit(cholesky)/cholesky | solution.py:18
  842.1 9.8 %custom-call.45 = f32[1,128,128]{1,2,0:T(8,128)S(1)} custom-call(f32[1,128,128]{2,1,0:T(8,128)S(1)} %get-tuple-element.11), custom_call_target="InvertDiagBlocksLowerTriangular" | custom-call | tf_op jit(solution)/shard_map/jit(cholesky)/cholesky | solution.py:18
  853.5 11.7 %cholesky.878 = f32[128,128]{1,0:T(8,128)S(1)} custom-call(f32[128,128]{1,0:T(8,128)S(1)} %cholesky.967), custom_call_target="Cholesky" | custom-call | tf_op jit(solution)/shard_map/jit(cholesky)/cholesky | solution.py:18
  865.9 9.8 %custom-call.46 = f32[1,128,128]{1,2,0:T(8,128)S(1)} custom-call(f32[1,128,128]{2,1,0:T(8,128)S(1)} %get-tuple-element.8), custom_call_target="InvertDiagBlocksLowerTriangular" | custom-call | tf_op jit(solution)/shard_map/jit(cholesky)/cholesky | solution.py:18
  877.4 11.7 %cholesky.895 = f32[128,128]{1,0:T(8,128)S(1)} custom-call(f32[128,128]{1,0:T(8,128)S(1)} %slice_subtract_fusion.10), custom_call_target="Cholesky" | custom-call | tf_op jit(solution)/shard_map/jit(cholesky)/cholesky | solution.py:18
  (128 shorter events, 67.8 us)
Async XLA Ops:
  0.6 1.4 copy-start
  57.2 32.5 %copy-start.6 = (f32[48,512]{1,0:T(8,128)}, f32[48,512]{1,0:T(8,128)S(1)}, u32[]{:S(2)}) copy-start(f32[48,512]{1,0:T(8,128)S(1)} %reduce_sum.9) | copy-start | bytes 294916
  58.2 4.6 collective-permute-start
  63.0 26.5 %collective-permute-start.1 = (f32[512,512]{0,1:T(8,128)S(1)}, f32[512,512]{0,1:T(8,128)S(1)}, u32[]{:S(2)}, u32[]{:S(2)}) collective-permute-start(f32[512,512]{0,1:T(8,128)S(1)} %add.60), channel_id=1, source_target_pairs={{0,2},{1,3},{2,0},{3,1},{4,6},{5,7},{6,4},{7,5},{8,10},{9,11},{10,... | collective-permute-start | bytes 3145736 | tf_op jit(solution)/shard_map/ppermute | solution.py:48
  89.7 27.1 %collective-permute-start.2 = (f32[512,512]{0,1:T(8,128)S(1)}, f32[512,512]{0,1:T(8,128)S(1)}, u32[]{:S(2)}, u32[]{:S(2)}) collective-permute-start(f32[512,512]{0,1:T(8,128)S(1)} %add.61), channel_id=1, source_target_pairs={{0,4},{1,5},{2,6},{3,7},{4,0},{5,1},{6,2},{7,3},{8,12},{9,13},{10,... | collective-permute-start | bytes 3145736 | tf_op jit(solution)/shard_map/ppermute | solution.py:48
  117.0 24.7 %collective-permute-start.3 = (f32[512,512]{0,1:T(8,128)S(1)}, f32[512,512]{0,1:T(8,128)S(1)}, u32[]{:S(2)}, u32[]{:S(2)}) collective-permute-start(f32[512,512]{0,1:T(8,128)S(1)} %add.62), channel_id=1, source_target_pairs={{0,8},{1,9},{2,10},{3,11},{4,12},{5,13},{6,14},{7,15},{8,0},{9,1},... | collective-permute-start | bytes 3145736 | tf_op jit(solution)/shard_map/ppermute | solution.py:48
  141.9 25.3 %collective-permute-start.4 = (f32[512,512]{0,1:T(8,128)S(1)}, f32[512,512]{0,1:T(8,128)S(1)}, u32[]{:S(2)}, u32[]{:S(2)}) collective-permute-start(f32[512,512]{0,1:T(8,128)S(1)} %add.63), channel_id=1, source_target_pairs={{0,16},{1,17},{2,18},{3,19},{4,20},{5,21},{6,22},{7,23},{8,24},{9,... | collective-permute-start | bytes 3145736 | tf_op jit(solution)/shard_map/ppermute | solution.py:48
  170.2 1.0 copy-start.5
  258.7 22.8 %collective-permute-start.5 = (f32[512,512]{0,1:T(8,128)S(1)}, f32[512,512]{0,1:T(8,128)S(1)}, u32[]{:S(2)}, u32[]{:S(2)}) collective-permute-start(f32[512,512]{0,1:T(8,128)S(1)} %fusion.24), channel_id=1, source_target_pairs={{0,32},{32,0},{64,96},{96,64},{128,160},{160,128},{192,224},{224,1... | collective-permute-start | bytes 3145736 | tf_op jit(solution)/shard_map/ppermute | solution.py:14
  286.1 1.0 copy-start.2
  375.2 50.2 %collective-permute-start.6 = (f32[512,512]{0,1:T(8,128)S(1)}, f32[512,512]{0,1:T(8,128)S(1)}, u32[]{:S(2)}, u32[]{:S(2)}) collective-permute-start(f32[512,512]{0,1:T(8,128)S(1)} %fusion.21), channel_id=1, source_target_pairs={{0,64},{64,0},{32,96},{96,32},{128,192},{192,128},{160,224},{224,1... | collective-permute-start | bytes 3145736 | tf_op jit(solution)/shard_map/ppermute | solution.py:14
  430.0 1.0 copy-start.3
  519.1 97.3 %collective-permute-start.7 = (f32[512,512]{0,1:T(8,128)S(1)}, f32[512,512]{0,1:T(8,128)S(1)}, u32[]{:S(2)}, u32[]{:S(2)}) collective-permute-start(f32[512,512]{0,1:T(8,128)S(1)} %fusion.18), channel_id=1, source_target_pairs={{0,128},{128,0},{32,160},{160,32},{64,192},{192,64},{96,224},{224,... | collective-permute-start | bytes 3145736 | tf_op jit(solution)/shard_map/ppermute | solution.py:14
  621.0 1.0 copy-start.4
  711.1 85.8 %collective-permute-start.8 = (f32[512,512]{0,1:T(8,128)}, f32[512,512]{0,1:T(8,128)}, u32[]{:S(2)}, u32[]{:S(2)}) collective-permute-start(f32[512,512]{0,1:T(8,128)} %fusion.15), channel_id=1, source_target_pairs={{0,256},{256,0},{32,288},{288,32},{64,320},{320,64},{96,352},{352,... | collective-permute-start | bytes 3145736 | tf_op jit(solution)/shard_map/ppermute | solution.py:14
  803.2 1.0 copy-start.1
